TPU v7x, 32 devices: a whole 2x2x4 slice. The times are simulated.
32 devices in a mesh: band: 2 (over y), slab: 16 (over z, x, core).
Axes of the slice: x: 2, y: 2, z: 4, core: 2. Of those that a mesh axis runs over, the one named last changes fastest.
Arguments:
- own_orbitals: float32 [4, 128, 128, 128], P('band', 'slab'), may hold values from -6 to 6
- partners: float32 [8, 128, 128, 128], P('band', 'slab'), may hold values from -6 to 6
Outputs:
- own_field: float32 [4, 128, 128, 128], P('band', 'slab')
- partner_field: float32 [8, 128, 128, 128], P('band', 'slab')
All inputs are finite; a program needn't handle non-finite values.
Results may differ from a plain program's by a relative error of at most 0.0001.
Values sent between devices are 32-bit elements; how exact they have to be, the bound alone decides.
No kernel may reach another device: no remote copies, remote signals or barrier semaphores. Data moves between devices by JAX's collectives and lax.ppermute only.
A program may use at most 128 MiB of HBM per device.

v0:
```python
import math
import jax
import jax.numpy as jnp
from jax import lax
from jax.sharding import PartitionSpec as P

STEPS = 2
coulomb_scale = 46.9 * 46.9 / math.pi
highest = lax.Precision.HIGHEST


def passed_along(block, axis, distance):
    devices = range(lax.axis_size(axis))
    route = [((i - distance) % len(devices), i) for i in devices]
    return lax.ppermute(block, axis, route)


def dft_tables(length):
    positions = lax.iota(jnp.int32, length)
    wrapped = positions[:, None] * positions[None, :] % length
    angles = wrapped.astype(jnp.float32) * (2.0 * math.pi / length)
    return (jnp.cos(angles), jnp.sin(angles))


def apply_table(pattern, field, table):
    return jnp.einsum(pattern, field, table, precision=highest)


def forward(pattern, real_part, imag_part, cosine, sine_table):
    new_real = apply_table(pattern, real_part, cosine) + apply_table(pattern, imag_part, sine_table)
    new_imag = apply_table(pattern, imag_part, cosine) - apply_table(pattern, real_part, sine_table)
    return (new_real, new_imag)


def inverse(pattern, real_part, imag_part, cosine, sine_table):
    new_real = apply_table(pattern, real_part, cosine) - apply_table(pattern, imag_part, sine_table)
    new_imag = apply_table(pattern, imag_part, cosine) + apply_table(pattern, real_part, sine_table)
    return (new_real, new_imag)


def frequency(positions, length):
    return jnp.where(positions < length // 2, positions, positions - length).astype(jnp.float32)


def shards(own_orbitals, partners):
    length = own_orbitals.shape[3]
    cosine, sine_table = dft_tables(length)
    slab_count = lax.axis_size("slab")
    rows_y = length // slab_count
    z_waves = frequency(lax.iota(jnp.int32, length), length)
    y_waves = frequency(lax.axis_index("slab") * rows_y + lax.iota(jnp.int32, rows_y), length)
    square = (
        z_waves[:, None, None] * z_waves[:, None, None]
        + y_waves[None, :, None] * y_waves[None, :, None]
        + z_waves[None, None, :] * z_waves[None, None, :]
    )
    kernel = jnp.where(square > 0, coulomb_scale / jnp.maximum(square, 1.0), 0.0) / float(
        length * length * length
    )
    x_form = "pzyx,xk->pzyk"
    y_form = "pzyx,yk->pzkx"
    z_form = "pzyx,zk->pkyx"
    own_acc = jnp.zeros(own_orbitals.shape, jnp.float32)
    partner_set = passed_along(partners, "band", 1)
    partner_out = jnp.zeros(partners.shape, jnp.float32)
    for step_no in range(1, STEPS + 1):
        if step_no > 1:
            partner_set = passed_along(partner_set, "band", 1)
        own_count = own_orbitals.shape[0]
        part_count = partner_set.shape[0]
        pair_count = own_count * part_count
        density = (own_orbitals[:, None] * partner_set[None]).reshape(
            (pair_count,) + own_orbitals.shape[1:]
        )
        potentials_real_part = apply_table(x_form, density, cosine)
        potentials_imag_part = -apply_table(x_form, density, sine_table)
        solve_real_part = potentials_real_part
        solve_imag_part = potentials_imag_part
        solve_real_part, solve_imag_part = forward(
            y_form, solve_real_part, solve_imag_part, cosine, sine_table
        )
        real_part, imag_part = forward(
            z_form,
            lax.all_to_all(solve_real_part, "slab", split_axis=2, concat_axis=1, tiled=True),
            lax.all_to_all(solve_imag_part, "slab", split_axis=2, concat_axis=1, tiled=True),
            cosine,
            sine_table,
        )
        real_part = real_part * kernel
        imag_part = imag_part * kernel
        real_part, imag_part = inverse(z_form, real_part, imag_part, cosine, sine_table)
        solve_real_part = lax.all_to_all(real_part, "slab", split_axis=1, concat_axis=2, tiled=True)
        solve_imag_part = lax.all_to_all(imag_part, "slab", split_axis=1, concat_axis=2, tiled=True)
        potentials_real_part, potentials_imag_part = inverse(
            y_form, solve_real_part, solve_imag_part, cosine, sine_table
        )
        potential = apply_table(x_form, potentials_real_part, cosine) - apply_table(
            x_form, potentials_imag_part, sine_table
        )
        potential = potential.reshape((own_count, part_count) + own_orbitals.shape[1:])
        own_add = jnp.sum(potential * partner_set[None], axis=1)
        part_add = jnp.sum(potential * own_orbitals[:, None], axis=0)
        own_add, part_add = (own_add, part_add)
        own_acc = own_acc + own_add
        partner_out = partner_out + passed_along(part_add, "band", -step_no)
    return (own_acc, partner_out)


def solution(mesh):
    in_specs = (P("band", "slab", None, None), P("band", "slab", None, None))
    out_specs = (P("band", "slab", None, None), P("band", "slab", None, None))
    return jax.shard_map(shards, mesh=mesh, in_specs=in_specs, out_specs=out_specs, check_vma=False)
```

profile of v0, /device:TPU:14, one launch (start us, length us, event | category | flops | bytes accessed | tf_op | source)
XLA Modules:
  0.0 983.0 jit_solution(5613835076587833565)
XLA Ops:
  1.2 47.1 %collective-permute-done = f32[4,8,128,128]{3,2,1,0:T(8,128)S(1)} collective-permute-done((f32[4,8,128,128]{3,2,1,0:T(8,128)}, f32[4,8,128,128]{3,2,1,0:T(8,128)S(1)}, u32[]{:S(2)}, u32[]{:S(2)}) %collective-permute-start) | collective-permute-done | bytes 2097184 | tf_op jit(solution)/shard_map/ppermute | solution.py:15
  48.8 46.0 %collective-permute-done.1 = f32[4,8,128,128]{3,2,1,0:T(8,128)S(1)} collective-permute-done((f32[4,8,128,128]{3,2,1,0:T(8,128)S(1)}, f32[4,8,128,128]{3,2,1,0:T(8,128)S(1)}, u32[]{:S(2)}, u32[]{:S(2)}) %collective-permute-start.1) | collective-permute-done | bytes 2097184 | tf_op jit(solution)/shard_map/ppermute | solution.py:15
  119.7 6.8 all-to-all-start.4
  126.5 6.1 fusion.125
  140.9 77.8 %all-to-all-done.4 = f32[8,8,128,128]{3,1,0,2:T(8,128)} async-done(((f32[8,8,128,128]{3,1,0,2:T(8,128)}), f32[8,8,128,128]{3,1,0,2:T(8,128)}, u32[]{:S(2)}, u32[]{:S(2)}) %all-to-all-start.4) | async-done | bytes 4194336 | tf_op jit(solution)/shard_map/all_to_all | solution.py:84
  223.7 6.0 fusion.161
  246.1 69.9 %all-to-all-done.5 = f32[8,8,128,128]{3,1,0,2:T(8,128)} async-done(((f32[8,8,128,128]{3,1,0,2:T(8,128)}), f32[8,8,128,128]{3,1,0,2:T(8,128)}, u32[]{:S(2)}, u32[]{:S(2)}) %all-to-all-start.5) | async-done | bytes 4194336 | tf_op jit(solution)/shard_map/all_to_all | solution.py:85
  321.1 6.1 fusion.163
  335.5 77.9 %all-to-all-done.1 = f32[8,8,128,128]{3,1,0,2:T(8,128)} async-done(((f32[8,8,128,128]{3,1,0,2:T(8,128)}), f32[8,8,128,128]{3,1,0,2:T(8,128)}, u32[]{:S(2)}, u32[]{:S(2)}) %all-to-all-start.1) | async-done | bytes 4194336 | tf_op jit(solution)/shard_map/all_to_all | solution.py:85
  425.3 6.0 fusion.18
  431.2 6.2 subtract_multiply_fusion
  443.5 6.3 add_multiply_fusion
  458.3 52.8 %all-to-all-done = f32[8,8,128,128]{3,1,0,2:T(8,128)} async-done(((f32[8,8,128,128]{3,1,0,2:T(8,128)}), f32[8,8,128,128]{3,1,0,2:T(8,128)}, u32[]{:S(2)}, u32[]{:S(2)}) %all-to-all-start) | async-done | bytes 4194336 | tf_op jit(solution)/shard_map/all_to_all | solution.py:84
  516.6 6.1 fusion.12
  531.1 77.6 %all-to-all-done.6 = f32[8,128,8,128]{3,2,0,1:T(8,128)} async-done(((f32[8,128,8,128]{3,2,0,1:T(8,128)}), f32[8,128,8,128]{3,2,0,1:T(8,128)}, u32[]{:S(2)}, u32[]{:S(2)}) %all-to-all-start.6) | async-done | bytes 4194336 | tf_op jit(solution)/shard_map/all_to_all | solution.py:92
  614.3 6.0 fusion.46
  626.3 6.2 subtract_multiply_fusion.1
  638.4 6.3 add_multiply_fusion.1
  653.3 53.2 %all-to-all-done.7 = f32[8,128,8,128]{3,2,0,1:T(8,128)} async-done(((f32[8,128,8,128]{3,2,0,1:T(8,128)}), f32[8,128,8,128]{3,2,0,1:T(8,128)}, u32[]{:S(2)}, u32[]{:S(2)}) %all-to-all-start.7) | async-done | bytes 4194336 | tf_op jit(solution)/shard_map/all_to_all | solution.py:93
  711.9 6.1 fusion.40
  726.4 77.6 %all-to-all-done.2 = f32[8,128,8,128]{3,2,0,1:T(8,128)} async-done(((f32[8,128,8,128]{3,2,0,1:T(8,128)}), f32[8,128,8,128]{3,2,0,1:T(8,128)}, u32[]{:S(2)}, u32[]{:S(2)}) %all-to-all-start.2) | async-done | bytes 4194336 | tf_op jit(solution)/shard_map/all_to_all | solution.py:92
  809.5 8.2 fusion.8
  817.7 8.1 fusion.10
  825.8 8.3 fusion.4
  834.2 8.2 fusion.6
  842.4 8.3 fusion.36
  850.7 8.4 fusion.38
  859.1 42.3 %all-to-all-done.3 = f32[8,128,8,128]{3,2,0,1:T(8,128)} async-done(((f32[8,128,8,128]{3,2,0,1:T(8,128)}), f32[8,128,8,128]{3,2,0,1:T(8,128)}, u32[]{:S(2)}, u32[]{:S(2)}) %all-to-all-start.3) | async-done | bytes 4194336 | tf_op jit(solution)/shard_map/all_to_all | solution.py:93
  901.4 6.0 fusion.32
  907.4 6.1 fusion.34
  921.3 6.0 multiply_reduce_fusion.2
  934.9 46.1 %collective-permute-done.2 = f32[4,8,128,128]{3,2,1,0:T(8,128)S(1)} collective-permute-done((f32[4,8,128,128]{3,2,1,0:T(8,128)S(1)}, f32[4,8,128,128]{3,2,1,0:T(8,128)S(1)}, u32[]{:S(2)}, u32[]{:S(2)}) %collective-permute-start.2) | collective-permute-done | bytes 2097184 | tf_op jit(solution)/shard_map/ppermute | solution.py:15
  (90 shorter events, 171.3 us)
Async XLA Ops:
  0.6 47.6 %collective-permute-start = (f32[4,8,128,128]{3,2,1,0:T(8,128)}, f32[4,8,128,128]{3,2,1,0:T(8,128)S(1)}, u32[]{:S(2)}, u32[]{:S(2)}) collective-permute-start(f32[4,8,128,128]{3,2,1,0:T(8,128)} %param.3), channel_id=1, source_target_pairs={{16,0},{0,16},{17,1},{1,17},{18,2},{2,18},{19,3},{3,19},{20,4},{4,... | collective-permute-start | bytes 6291464 | tf_op jit(solution)/shard_map/ppermute | solution.py:15
  48.3 46.5 %collective-permute-start.1 = (f32[4,8,128,128]{3,2,1,0:T(8,128)S(1)}, f32[4,8,128,128]{3,2,1,0:T(8,128)S(1)}, u32[]{:S(2)}, u32[]{:S(2)}) collective-permute-start(f32[4,8,128,128]{3,2,1,0:T(8,128)S(1)} %collective-permute-done), channel_id=1, source_target_pairs={{16,0},{0,16},{17,1},{1,17},{18,2},{2,18},{19,3},{3,19},{20,4},{4,... | collective-permute-start | bytes 6291464 | tf_op jit(solution)/shard_map/ppermute | solution.py:15
  94.8 4.7 copy-start.19
  103.3 3.7 copy-start.12
  107.0 8.3 copy-start.6
  119.7 99.0 %all-to-all-start.4 = ((f32[8,8,128,128]{3,1,0,2:T(8,128)}), f32[8,8,128,128]{3,1,0,2:T(8,128)}, u32[]{:S(2)}, u32[]{:S(2)}) async-start(f32[8,8,128,128]{3,1,0,2:T(8,128)} %copy.136), calls=%async_computation.4 | async-start | bytes 8388608 | tf_op jit(solution)/shard_map/all_to_all | solution.py:84
  126.5 6.1 copy-start.7
  218.6 97.4 %all-to-all-start.5 = ((f32[8,8,128,128]{3,1,0,2:T(8,128)}), f32[8,8,128,128]{3,1,0,2:T(8,128)}, u32[]{:S(2)}, u32[]{:S(2)}) async-start(f32[8,8,128,128]{3,1,0,2:T(8,128)} %copy.141), calls=%async_computation.5 | async-start | bytes 8388608 | tf_op jit(solution)/shard_map/all_to_all | solution.py:85
  223.7 6.0 copy-start.10
  229.7 3.7 copy-start.11
  233.4 4.1 copy-start.4
  316.0 97.4 %all-to-all-start.1 = ((f32[8,8,128,128]{3,1,0,2:T(8,128)}), f32[8,8,128,128]{3,1,0,2:T(8,128)}, u32[]{:S(2)}, u32[]{:S(2)}) async-start(f32[8,8,128,128]{3,1,0,2:T(8,128)} %copy.115), calls=%async_computation.1 | async-start | bytes 8388608 | tf_op jit(solution)/shard_map/all_to_all | solution.py:85
  321.1 6.1 copy-start.5
  413.4 97.8 %all-to-all-start = ((f32[8,8,128,128]{3,1,0,2:T(8,128)}), f32[8,8,128,128]{3,1,0,2:T(8,128)}, u32[]{:S(2)}, u32[]{:S(2)}) async-start(f32[8,8,128,128]{3,1,0,2:T(8,128)} %copy.110), calls=%async_computation | async-start | bytes 8388608 | tf_op jit(solution)/shard_map/all_to_all | solution.py:84
  437.4 2.0 copy-start.9
  449.8 4.1 copy-start.2
  511.2 97.6 %all-to-all-start.6 = ((f32[8,128,8,128]{3,2,0,1:T(8,128)}), f32[8,128,8,128]{3,2,0,1:T(8,128)}, u32[]{:S(2)}, u32[]{:S(2)}) async-start(f32[8,128,8,128]{3,2,0,1:T(8,128)} %copy.148), calls=%async_computation.6 | async-start | bytes 8388608 | tf_op jit(solution)/shard_map/all_to_all | solution.py:92
  516.6 6.1 copy-start.3
  608.7 97.8 %all-to-all-start.7 = ((f32[8,128,8,128]{3,2,0,1:T(8,128)}), f32[8,128,8,128]{3,2,0,1:T(8,128)}, u32[]{:S(2)}, u32[]{:S(2)}) async-start(f32[8,128,8,128]{3,2,0,1:T(8,128)} %copy.154), calls=%async_computation.7 | async-start | bytes 8388608 | tf_op jit(solution)/shard_map/all_to_all | solution.py:93
  644.7 4.1 copy-start
  706.5 97.6 %all-to-all-start.2 = ((f32[8,128,8,128]{3,2,0,1:T(8,128)}), f32[8,128,8,128]{3,2,0,1:T(8,128)}, u32[]{:S(2)}, u32[]{:S(2)}) async-start(f32[8,128,8,128]{3,2,0,1:T(8,128)} %copy.122), calls=%async_computation.2 | async-start | bytes 8388608 | tf_op jit(solution)/shard_map/all_to_all | solution.py:92
  711.9 6.1 copy-start.1
  804.1 97.4 %all-to-all-start.3 = ((f32[8,128,8,128]{3,2,0,1:T(8,128)}), f32[8,128,8,128]{3,2,0,1:T(8,128)}, u32[]{:S(2)}, u32[]{:S(2)}) async-start(f32[8,128,8,128]{3,2,0,1:T(8,128)} %copy.128), calls=%async_computation.3 | async-start | bytes 8388608 | tf_op jit(solution)/shard_map/all_to_all | solution.py:93
  907.4 6.2 copy-start.16
  907.4 6.2 copy-start.17
  913.6 3.9 copy-start.18
  917.4 3.9 copy-start.14
  917.4 3.9 copy-start.15
  921.3 6.0 copy-start.13
  927.3 4.4 copy-start.20
  933.1 47.9 %collective-permute-start.2 = (f32[4,8,128,128]{3,2,1,0:T(8,128)S(1)}, f32[4,8,128,128]{3,2,1,0:T(8,128)S(1)}, u32[]{:S(2)}, u32[]{:S(2)}) collective-permute-start(f32[4,8,128,128]{3,2,1,0:T(8,128)S(1)} %get-tuple-element.3), channel_id=1, source_target_pairs={{16,0},{0,16},{17,1},{1,17},{18,2},{2,18},{19,3},{3,19},{20,4},{4,... | collective-permute-start | bytes 6291464 | tf_op jit(solution)/shard_map/ppermute | solution.py:15
  933.7 47.3 %collective-permute-start.3 = (f32[4,8,128,128]{3,2,1,0:T(8,128)S(1)}, f32[4,8,128,128]{3,2,1,0:T(8,128)S(1)}, u32[]{:S(2)}, u32[]{:S(2)}) collective-permute-start(f32[4,8,128,128]{3,2,1,0:T(8,128)S(1)} %get-tuple-element.2), channel_id=1, source_target_pairs={{0,0},{16,16},{1,1},{17,17},{2,2},{18,18},{3,3},{19,19},{4,4},{20,... | collective-permute-start | bytes 6291464 | tf_op jit(solution)/shard_map/ppermute | solution.py:15
  (1 other events, 1.9 us)
where the time goes:
time: 992 us; the launch traced here: 983 us
  waiting for transfers between devices  668 us (67%)
  matrix products  218 us (22%)
  starting transfers between devices  46.1 us (5%)
  local copies, waits for them, and re-layouts  39.5 us (4%)
    dot_general x40, matrix products, apply_table(): return jnp.einsum(pattern, field, table, precision=highest)  218 us
    all_to_all x2, waiting for transfers between devices, shards(): lax.all_to_all(real_part, 'slab', split_axis=1, concat_axis=2, tiled=True)  155 us
    all_to_all x2, waiting for transfers between devices, shards(): lax.all_to_all(solve_imag_part, 'slab', split_axis=2, concat_axis=1, tile...  148 us
    ppermute x4, waiting for transfers between devices, passed_along(): return lax.ppermute(block, axis, route)  139 us
    all_to_all x2, waiting for transfers between devices, shards(): lax.all_to_all(solve_real_part, 'slab', split_axis=2, concat_axis=1, tile...  131 us
    all_to_all x2, waiting for transfers between devices, shards(): lax.all_to_all(imag_part, 'slab', split_axis=1, concat_axis=2, tiled=True)  95.5 us
  transfers between devices with their start and end apart: 12, of which 11 were waited for; matrix products, arithmetic and copies ran while one was open for 21% of the time, Pallas kernels for 0%

commit v1 on v0

--- a/solution.py
+++ b/solution.py
@@ -82,7 +82,15 @@
         real_part, imag_part = forward(
             z_form,
             lax.all_to_all(solve_real_part, "slab", split_axis=2, concat_axis=1, tiled=True),
-            lax.all_to_all(solve_imag_part, "slab", split_axis=2, concat_axis=1, tiled=True),
+            jnp.concatenate(
+                lax.all_to_all(
+                    jnp.stack(jnp.split(solve_imag_part, lax.axis_size("slab"), axis=2)),
+                    "slab",
+                    0,
+                    0,
+                ),
+                axis=1,
+            ),
             cosine,
             sine_table,
         )

time: 992 us -> 997 us (level)
  local copies, waits for them, and re-layouts: 39.5 us -> 59.9 us
    unnamed x42 -> x76, local copies, waits for them, and re-layouts: 4.03 us -> 26.6 us
    all_to_all x2, waiting for transfers between devices: 131 us -> 115 us  [shards(): lax.all_to_all(solve_real_part, 'slab', split_axis=2, concat_axis=1, tile...]
  transfers between devices with their start and end apart: 12 -> 12, of which waited for: 11 -> 11; matrix products, arithmetic and copies ran while one was open for 21% -> 22% of each run, Pallas kernels for 0% -> 0%
where the time goes in v1:
time: 997 us; the launch traced here: 987 us
  waiting for transfers between devices  660 us (66%)
  matrix products  213 us (21%)
  local copies, waits for them, and re-layouts  59.9 us (6%)
  starting transfers between devices  44.2 us (4%)
    dot_general x40, matrix products, apply_table(): return jnp.einsum(pattern, field, table, precision=highest)  213 us
    all_to_all x2, waiting for transfers between devices, shards(): lax.all_to_all(jnp.stack(jnp.split(solve_imag_part, lax.axis_size('slab')...  156 us
    all_to_all x2, waiting for transfers between devices, shards(): lax.all_to_all(real_part, 'slab', split_axis=1, concat_axis=2, tiled=True)  155 us
    ppermute x4, waiting for transfers between devices, passed_along(): return lax.ppermute(block, axis, route)  139 us
    all_to_all x2, waiting for transfers between devices, shards(): lax.all_to_all(solve_real_part, 'slab', split_axis=2, concat_axis=1, tile...  115 us
    all_to_all x2, waiting for transfers between devices, shards(): lax.all_to_all(imag_part, 'slab', split_axis=1, concat_axis=2, tiled=True)  95.3 us
    unnamed x76, local copies, waits for them, and re-layouts  26.6 us
  transfers between devices with their start and end apart: 12, of which 11 were waited for; matrix products, arithmetic and copies ran while one was open for 22% of the time, Pallas kernels for 0%

profile of v1, /device:TPU:14, one launch (start us, length us, event | category | flops | bytes accessed | tf_op | source)
XLA Modules:
  0.0 987.4 jit_solution(18206243054293118948)
XLA Ops:
  1.2 47.1 %collective-permute-done = f32[4,8,128,128]{3,2,1,0:T(8,128)S(1)} collective-permute-done((f32[4,8,128,128]{3,2,1,0:T(8,128)}, f32[4,8,128,128]{3,2,1,0:T(8,128)S(1)}, u32[]{:S(2)}, u32[]{:S(2)}) %collective-permute-start) | collective-permute-done | bytes 2097184 | tf_op jit(solution)/shard_map/ppermute | solution.py:15
  48.8 46.0 %collective-permute-done.1 = f32[4,8,128,128]{3,2,1,0:T(8,128)S(1)} collective-permute-done((f32[4,8,128,128]{3,2,1,0:T(8,128)S(1)}, f32[4,8,128,128]{3,2,1,0:T(8,128)S(1)}, u32[]{:S(2)}, u32[]{:S(2)}) %collective-permute-start.1) | collective-permute-done | bytes 2097184 | tf_op jit(solution)/shard_map/ppermute | solution.py:15
  126.4 6.2 all-to-all-start.5
  132.6 6.1 fusion.176
  147.0 77.9 %all-to-all-done.5 = f32[16,8,8,8,128]{4,3,2,1,0:T(8,128)} async-done(((f32[16,8,8,8,128]{4,3,2,1,0:T(8,128)}), f32[16,8,8,8,128]{4,3,2,1,0:T(8,128)}, u32[]{:S(2)}, u32[]{:S(2)}) %all-to-all-start.5) | async-done | bytes 4194336 | tf_op jit(solution)/shard_map/all_to_all | solution.py:86
  230.0 6.3 fusion.189
  260.1 62.2 %all-to-all-done.4 = f32[8,8,128,128]{3,1,0,2:T(8,128)} async-done(((f32[8,8,128,128]{3,1,0,2:T(8,128)}), f32[8,8,128,128]{3,1,0,2:T(8,128)}, u32[]{:S(2)}, u32[]{:S(2)}) %all-to-all-start.4) | async-done | bytes 4194336 | tf_op jit(solution)/shard_map/all_to_all | solution.py:84
  327.4 6.1 fusion.191
  341.8 77.9 %all-to-all-done.1 = f32[16,8,8,8,128]{4,3,2,1,0:T(8,128)} async-done(((f32[16,8,8,8,128]{4,3,2,1,0:T(8,128)}), f32[16,8,8,8,128]{4,3,2,1,0:T(8,128)}, u32[]{:S(2)}, u32[]{:S(2)}) %all-to-all-start.1) | async-done | bytes 4194336 | tf_op jit(solution)/shard_map/all_to_all | solution.py:86
  427.8 6.0 fusion.18
  433.8 6.2 fusion.16
  464.4 52.6 %all-to-all-done = f32[8,8,128,128]{3,1,0,2:T(8,128)} async-done(((f32[8,8,128,128]{3,1,0,2:T(8,128)}), f32[8,8,128,128]{3,1,0,2:T(8,128)}, u32[]{:S(2)}, u32[]{:S(2)}) %all-to-all-start) | async-done | bytes 4194336 | tf_op jit(solution)/shard_map/all_to_all | solution.py:84
  517.0 5.4 all-to-all-start.6
  522.4 6.1 fusion.12
  537.0 77.6 %all-to-all-done.6 = f32[8,128,8,128]{3,2,0,1:T(8,128)} async-done(((f32[8,128,8,128]{3,2,0,1:T(8,128)}), f32[8,128,8,128]{3,2,0,1:T(8,128)}, u32[]{:S(2)}, u32[]{:S(2)}) %all-to-all-start.6) | async-done | bytes 4194336 | tf_op jit(solution)/shard_map/all_to_all | solution.py:100
  622.4 6.0 fusion.42
  628.4 6.2 fusion.40
  658.9 53.1 %all-to-all-done.7 = f32[8,128,8,128]{3,2,0,1:T(8,128)} async-done(((f32[8,128,8,128]{3,2,0,1:T(8,128)}), f32[8,128,8,128]{3,2,0,1:T(8,128)}, u32[]{:S(2)}, u32[]{:S(2)}) %all-to-all-start.7) | async-done | bytes 4194336 | tf_op jit(solution)/shard_map/all_to_all | solution.py:101
  712.0 5.4 all-to-all-start.2
  717.3 6.1 fusion.36
  731.9 77.6 %all-to-all-done.2 = f32[8,128,8,128]{3,2,0,1:T(8,128)} async-done(((f32[8,128,8,128]{3,2,0,1:T(8,128)}), f32[8,128,8,128]{3,2,0,1:T(8,128)}, u32[]{:S(2)}, u32[]{:S(2)}) %all-to-all-start.2) | async-done | bytes 4194336 | tf_op jit(solution)/shard_map/all_to_all | solution.py:100
  809.5 5.2 all-to-all-start.3
  814.7 8.2 fusion.8
  823.0 8.1 fusion.10
  831.1 8.6 fusion.4
  839.7 8.2 fusion.6
  847.9 8.3 fusion.32
  856.1 8.4 fusion.34
  864.6 42.3 %all-to-all-done.3 = f32[8,128,8,128]{3,2,0,1:T(8,128)} async-done(((f32[8,128,8,128]{3,2,0,1:T(8,128)}), f32[8,128,8,128]{3,2,0,1:T(8,128)}, u32[]{:S(2)}, u32[]{:S(2)}) %all-to-all-start.3) | async-done | bytes 4194336 | tf_op jit(solution)/shard_map/all_to_all | solution.py:101
  906.9 6.0 fusion.28
  912.9 6.1 fusion.30
  939.4 46.1 %collective-permute-done.2 = f32[4,8,128,128]{3,2,1,0:T(8,128)S(1)} collective-permute-done((f32[4,8,128,128]{3,2,1,0:T(8,128)S(1)}, f32[4,8,128,128]{3,2,1,0:T(8,128)S(1)}, u32[]{:S(2)}, u32[]{:S(2)}) %collective-permute-start.2) | collective-permute-done | bytes 2097184 | tf_op jit(solution)/shard_map/ppermute | solution.py:15
  (126 shorter events, 186.5 us)
Async XLA Ops:
  0.6 47.6 %collective-permute-start = (f32[4,8,128,128]{3,2,1,0:T(8,128)}, f32[4,8,128,128]{3,2,1,0:T(8,128)S(1)}, u32[]{:S(2)}, u32[]{:S(2)}) collective-permute-start(f32[4,8,128,128]{3,2,1,0:T(8,128)} %param.3), channel_id=1, source_target_pairs={{16,0},{0,16},{17,1},{1,17},{18,2},{2,18},{19,3},{3,19},{20,4},{4,... | collective-permute-start | bytes 6291464 | tf_op jit(solution)/shard_map/ppermute | solution.py:15
  48.3 50.5 %copy-start.19 = (f32[4,8,128,128]{3,2,1,0:T(8,128)}, f32[4,8,128,128]{3,2,1,0:T(8,128)S(1)}, u32[]{:S(2)}) copy-start(f32[4,8,128,128]{3,2,1,0:T(8,128)S(1)} %collective-permute-done) | copy-start | bytes 6291460
  48.3 46.5 %collective-permute-start.1 = (f32[4,8,128,128]{3,2,1,0:T(8,128)S(1)}, f32[4,8,128,128]{3,2,1,0:T(8,128)S(1)}, u32[]{:S(2)}, u32[]{:S(2)}) collective-permute-start(f32[4,8,128,128]{3,2,1,0:T(8,128)S(1)} %collective-permute-done), channel_id=1, source_target_pairs={{16,0},{0,16},{17,1},{1,17},{18,2},{2,18},{19,3},{3,19},{20,4},{4,... | collective-permute-start | bytes 6291464 | tf_op jit(solution)/shard_map/ppermute | solution.py:15
  102.6 3.7 copy-start.12
  106.3 8.2 copy-start.6
  126.4 98.6 %all-to-all-start.5 = ((f32[16,8,8,8,128]{4,3,2,1,0:T(8,128)}), f32[16,8,8,8,128]{4,3,2,1,0:T(8,128)}, u32[]{:S(2)}, u32[]{:S(2)}) async-start(f32[16,8,8,8,128]{4,3,2,1,0:T(8,128)} %fusion.113), calls=%async_computation.5 | async-start | bytes 8388608 | tf_op jit(solution)/shard_map/all_to_all | solution.py:86
  132.6 6.1 copy-start.7
  224.9 97.4 %all-to-all-start.4 = ((f32[8,8,128,128]{3,1,0,2:T(8,128)}), f32[8,8,128,128]{3,1,0,2:T(8,128)}, u32[]{:S(2)}, u32[]{:S(2)}) async-start(f32[8,8,128,128]{3,1,0,2:T(8,128)} %copy.141), calls=%async_computation.4 | async-start | bytes 8388608 | tf_op jit(solution)/shard_map/all_to_all | solution.py:84
  230.0 6.3 copy-start.10
  236.3 3.7 copy-start.11
  240.0 4.1 copy-start.4
  322.3 97.4 %all-to-all-start.1 = ((f32[16,8,8,8,128]{4,3,2,1,0:T(8,128)}), f32[16,8,8,8,128]{4,3,2,1,0:T(8,128)}, u32[]{:S(2)}, u32[]{:S(2)}) async-start(f32[16,8,8,8,128]{4,3,2,1,0:T(8,128)} %fusion.129), calls=%async_computation.1 | async-start | bytes 8388608 | tf_op jit(solution)/shard_map/all_to_all | solution.py:86
  327.4 6.1 copy-start.5
  419.7 97.4 %all-to-all-start = ((f32[8,8,128,128]{3,1,0,2:T(8,128)}), f32[8,8,128,128]{3,1,0,2:T(8,128)}, u32[]{:S(2)}, u32[]{:S(2)}) async-start(f32[8,8,128,128]{3,1,0,2:T(8,128)} %copy.114), calls=%async_computation | async-start | bytes 8388608 | tf_op jit(solution)/shard_map/all_to_all | solution.py:84
  455.9 4.1 copy-start.2
  517.0 97.5 %all-to-all-start.6 = ((f32[8,128,8,128]{3,2,0,1:T(8,128)}), f32[8,128,8,128]{3,2,0,1:T(8,128)}, u32[]{:S(2)}, u32[]{:S(2)}) async-start(f32[8,128,8,128]{3,2,0,1:T(8,128)} %copy.154), calls=%async_computation.6 | async-start | bytes 8388608 | tf_op jit(solution)/shard_map/all_to_all | solution.py:100
  522.4 6.1 copy-start.3
  614.6 97.4 %all-to-all-start.7 = ((f32[8,128,8,128]{3,2,0,1:T(8,128)}), f32[8,128,8,128]{3,2,0,1:T(8,128)}, u32[]{:S(2)}, u32[]{:S(2)}) async-start(f32[8,128,8,128]{3,2,0,1:T(8,128)} %copy.160), calls=%async_computation.7 | async-start | bytes 8388608 | tf_op jit(solution)/shard_map/all_to_all | solution.py:101
  650.5 4.1 copy-start
  712.0 97.5 %all-to-all-start.2 = ((f32[8,128,8,128]{3,2,0,1:T(8,128)}), f32[8,128,8,128]{3,2,0,1:T(8,128)}, u32[]{:S(2)}, u32[]{:S(2)}) async-start(f32[8,128,8,128]{3,2,0,1:T(8,128)} %copy.127), calls=%async_computation.2 | async-start | bytes 8388608 | tf_op jit(solution)/shard_map/all_to_all | solution.py:100
  717.3 6.1 copy-start.1
  809.5 97.4 %all-to-all-start.3 = ((f32[8,128,8,128]{3,2,0,1:T(8,128)}), f32[8,128,8,128]{3,2,0,1:T(8,128)}, u32[]{:S(2)}, u32[]{:S(2)}) async-start(f32[8,128,8,128]{3,2,0,1:T(8,128)} %copy.133), calls=%async_computation.3 | async-start | bytes 8388608 | tf_op jit(solution)/shard_map/all_to_all | solution.py:101
  912.8 6.2 copy-start.16
  912.8 6.2 copy-start.17
  919.0 3.9 copy-start.18
  922.9 3.9 copy-start.14
  922.9 3.9 copy-start.15
  926.8 5.0 copy-start.13
  926.8 5.0 copy-start.20
  931.8 4.3 copy-start.22
  937.6 47.9 %collective-permute-start.2 = (f32[4,8,128,128]{3,2,1,0:T(8,128)S(1)}, f32[4,8,128,128]{3,2,1,0:T(8,128)S(1)}, u32[]{:S(2)}, u32[]{:S(2)}) collective-permute-start(f32[4,8,128,128]{3,2,1,0:T(8,128)S(1)} %get-tuple-element.3), channel_id=1, source_target_pairs={{16,0},{0,16},{17,1},{1,17},{18,2},{2,18},{19,3},{3,19},{20,4},{4,... | collective-permute-start | bytes 6291464 | tf_op jit(solution)/shard_map/ppermute | solution.py:15
  938.2 47.3 %collective-permute-start.3 = (f32[4,8,128,128]{3,2,1,0:T(8,128)S(1)}, f32[4,8,128,128]{3,2,1,0:T(8,128)S(1)}, u32[]{:S(2)}, u32[]{:S(2)}) collective-permute-start(f32[4,8,128,128]{3,2,1,0:T(8,128)S(1)} %get-tuple-element.2), channel_id=1, source_target_pairs={{0,0},{16,16},{1,1},{17,17},{2,2},{18,18},{3,3},{19,19},{4,4},{20,... | collective-permute-start | bytes 6291464 | tf_op jit(solution)/shard_map/ppermute | solution.py:15
  (3 other events, 6.2 us)
